TPU v7x, 32 devices: a whole 2x2x4 slice. The times are simulated.
32 devices in a mesh: grp: 2 (over y), skill: 16 (over z, x, core).
Axes of the slice: x: 2, y: 2, z: 4, core: 2. Of those that a mesh axis runs over, the one named last changes fastest.
Arguments:
- value_next: bfloat16 [2048, 4, 2048], P('skill', 'grp'), parts along dimension 1, may hold values from -6 to 6
- income_matrix: float32 [64, 32], P('grp'), parts along dimension 0, may hold values from -1 to 1
- block_weights: bfloat16 [16, 16, 4, 128, 128], P('skill')
- block_offset: int32 [16, 16, 4], P('skill'), may hold values from 0 to 3, as said below
- block_count: int32 [16, 16], P('skill'), may hold values from 1 to 4, as said below
- asset_next: int32 [16, 2, 2048], replicated, may hold values from 0 to 1
- flow: float32 [32, 2, 2048], P('grp'), parts along dimension 0, may hold values from -4 to 15
Outputs:
- value_now: bfloat16 [2048, 4, 2048], P('skill', 'grp'), parts along dimension 1
There are 2 independent parts, one for each index of `grp`. A program takes and returns all parts, laid end to end along the dimension named above; an argument that names none is the same for every part. Nothing has to cross between parts.
Inputs may be any that keep to these rules, and one draw needn't show every extreme that they name: `block_offset`: each row of 4 entries is a permutation of 0 to 3, the same for every level. `block_count`: the same for every level.
All inputs are finite; a program needn't handle non-finite values.
Results may differ from a plain program's by a relative error of at most 0.0031.
Values may be sent and summed in bfloat16 or wider, within the bound.
A program may use at most 128 MiB of HBM per device.

v0:
```python
import jax
import jax.numpy as jnp
from jax import lax
from jax.sharding import PartitionSpec as P


def shifted(block, axis, distance):
    devices = range(lax.axis_size(axis))
    route = [(i - distance, i) for i in devices if i - distance in devices]
    return lax.ppermute(block, axis, route)


def on_device(
    value_next, income_matrix, block_weights, block_offset, block_count, asset_next, flow
):
    tiles = lax.axis_size("skill")
    local_rows, assets, skills = value_next.shape
    tile = skills // tiles
    rows = local_rows * tiles
    shocks = income_matrix.shape[0]
    parents = rows // shocks
    blocks = block_offset.shape[-1]
    levels = block_offset.shape[1]
    arrived = lax.all_to_all(value_next, "skill", split_axis=2, concat_axis=0, tiled=True)
    width = arrived.shape[2]
    grid = arrived.astype(jnp.float32).reshape(parents, shocks, assets * width)
    mixed = jnp.einsum("fe,hex->hfx", income_matrix, grid, precision=lax.Precision.HIGHEST)
    own_tile = mixed.reshape(rows, assets, width).astype(jnp.bfloat16)
    gathered = [own_tile]
    for step in range(1, blocks):
        gathered.append(shifted(own_tile, "skill", -step))
    window = jnp.concatenate(gathered, axis=2)
    matrix = window.reshape(rows * assets, blocks * tile)
    place = jnp.arange(blocks, dtype=jnp.int32)
    offsets = block_offset[0]
    counts = block_count[0]
    select = (
        (offsets[:, :, None] == place[None, None, :])
        & (place[None, :, None] < counts[:, None, None])
    ).astype(jnp.float32)
    transit = jnp.einsum("ikr,ikst->irts", select, block_weights[0].astype(jnp.float32))
    transit = transit.astype(jnp.bfloat16).reshape(levels, blocks * tile, tile)
    flow_rows = jnp.transpose(flow, (0, 2, 1))[..., None]
    choose = jnp.transpose(asset_next, (0, 2, 1))

    def level_step(index, carry):
        running_max, running_total = carry
        cont = jnp.dot(matrix, transit[index], preferred_element_type=jnp.float32).reshape(
            rows, assets, tile
        )
        chosen = choose[index][:, :, None]
        picked = jnp.zeros((rows, assets, tile), jnp.float32)
        for option in range(assets):
            picked = picked + jnp.where(chosen == option, cont[:, option : option + 1, :], 0.0)
        score = (flow_rows[index] + 0.96 * picked) / 0.05
        new_max = jnp.maximum(running_max, score)
        new_total = running_total * jnp.exp(running_max - new_max) + jnp.exp(score - new_max)
        return (new_max, new_total)

    start_max = jnp.full((rows, assets, tile), -jnp.inf, jnp.float32)
    start_total = jnp.zeros((rows, assets, tile), jnp.float32)
    final_max, final_total = lax.fori_loop(0, levels, level_step, (start_max, start_total))
    value_tile = (0.05 * (final_max + jnp.log(final_total))).astype(jnp.bfloat16)
    return lax.all_to_all(value_tile, "skill", split_axis=0, concat_axis=2, tiled=True)


def solution(mesh):
    placed = (
        P("skill", "grp", None),
        P("grp", None),
        P("skill", None, None, None, None),
        P("skill", None, None),
        P("skill", None),
        P(),
        P("grp", None, None),
    )
    return jax.shard_map(
        on_device, mesh=mesh, in_specs=placed, out_specs=P("skill", "grp", None), check_vma=False
    )
```

profile of v0, /device:TPU:1, one launch (start us, length us, event | category | flops | bytes accessed | tf_op | source)
XLA Modules:
  0.0 645.9 jit_solution(14439508790451273633)
XLA Ops:
  0.0 4.9 copy.39
  4.9 32.5 %all_to_all.33 = bf16[128,2,2048]{0,1,2:T(2,128)(2,1)S(1)} all-to-all(bf16[128,2,2048]{0,1,2:T(2,128)(2,1)} %copy.39), channel_id=1, replica_groups=mesh['grp'=2,'skill'=16] {'skill'}, dimensions={2} | all-to-all | bytes 2097152 | tf_op jit(solution)/shard_map/all_to_all | solution.py:24
  54.1 4.2 copy.44
  58.3 8.6 %copy.36 = s32[16,2,2048]{1,2,0:T(8,128)} copy(s32[16,2,2048]{2,1,0:T(2,128)S(1)} %copy-done.3) | data formatting | bytes 524288 | tf_op args[5]
  66.9 8.6 %copy.35 = f32[16,2,2048]{1,2,0:T(8,128)} copy(f32[16,2,2048]{2,1,0:T(2,128)S(1)} %copy-done.4) | data formatting | bytes 524288 | tf_op args[6]
  75.5 17.9 %collective-permute-done.1 = bf16[2048,2,128]{2,1,0:T(2,128)(2,1)} collective-permute-done((bf16[2048,2,128]{2,1,0:T(2,128)(2,1)S(1)}, bf16[2048,2,128]{2,1,0:T(2,128)(2,1)}, u32[]{:S(2)}, u32[]{:S(2)}) %collective-permute-start.1) | collective-permute-done | bytes 1048608 | tf_op jit(solution)/shard_map/ppermute | solution.py:10
  95.2 8.8 %pad_maximum_fusion = bf16[2048,2,512]{2,1,0:T(2,128)(2,1)} fusion(bf16[2048,2,128]{2,1,0:T(2,128)(2,1)} %collective-permute-done.2, bf16[2048,2,128]{2,1,0:T(2,128)(2,1)} %collective-permute-done.1, bf16[2048,2,128]{2,1,0:T(2,128)(2,1)} %collective-permute-done, bf16[2048,2,128]{2,1,0:T(2,128)(2,1)S(1)} %convert_element_type.25), kind=kLoop, calls=%fused_computation.12 | loop fusion | flops 16777216 | bytes 8388608 | tf_op jit(solution)/shard_map/concatenate | solution.py:32
  103.9 7.2 %reshape.73 = bf16[4096,512]{1,0:T(8,128)(2,1)} reshape(bf16[2048,2,512]{2,1,0:T(2,128)(2,1)} %pad_maximum_fusion) | data formatting | bytes 8388608 | tf_op jit(solution)/shard_map/reshape | solution.py:33
  111.1 487.8 %while.16 = (s32[]{:T(128)}, f32[2048,2,128]{2,1,0:T(2,128)}, f32[2048,2,128]{2,1,0:T(2,128)}, f32[16,2048,2,1]{2,1,3,0:T(8,128)}, s32[16,2048,2]{2,1,0:T(8,128)...) while((s32[]{:T(128)}, f32[2048,2,128]{2,1,0:T(2,128)}, ...), condition=%wide.region_1.2_spmd.clone, body=%wide.region_0.1_spmd.clone.sunk | while | flops 543694848 | bytes 25395352 | solution.py:62
  120.2 3.9 fusion.26
  124.1 16.8 %fusion.27 = (f32[2048,2,128]{2,1,0:T(2,128)}, f32[2048,2,128]{2,1,0:T(2,128)}) fusion(f32[2048,2,128]{2,1,0:T(2,128)} %get-tuple-element.270, pred[]{:T(512)S(6)} %compare.3, f32[2048,2,128]{2,1,0:T(2,128)} %get-tuple-element.269, f32[2048,128]{1,0:T(8,128)S(1)} %bitcast.63, pred[2048,2]{1,0:T(8,128)(4,1)S(1)} %copy-done.2, ...), kind=kLoop, calls=%fused_computation.2.clone.1 | loop fusion | flops 6815744 | bytes 10510337 | tf_op jit(solution)/shard_map/while/body/eval_jaxpr/add | solution.py:57
  144.5 3.8 convolution_bitcast_fusion.2
  150.1 3.9 fusion.26
  154.0 17.5 %fusion.27 = (f32[2048,2,128]{2,1,0:T(2,128)}, f32[2048,2,128]{2,1,0:T(2,128)}) fusion(f32[2048,2,128]{2,1,0:T(2,128)} %get-tuple-element.270, pred[]{:T(512)S(6)} %compare.3, f32[2048,2,128]{2,1,0:T(2,128)} %get-tuple-element.269, f32[2048,128]{1,0:T(8,128)S(1)} %bitcast.63, pred[2048,2]{1,0:T(8,128)(4,1)S(1)} %copy-done.2, ...), kind=kLoop, calls=%fused_computation.2.clone.1 | loop fusion | flops 6815744 | bytes 10510337 | tf_op jit(solution)/shard_map/while/body/eval_jaxpr/add | solution.py:57
  180.6 3.9 fusion.26
  184.5 17.5 %fusion.27 = (f32[2048,2,128]{2,1,0:T(2,128)}, f32[2048,2,128]{2,1,0:T(2,128)}) fusion(f32[2048,2,128]{2,1,0:T(2,128)} %get-tuple-element.270, pred[]{:T(512)S(6)} %compare.3, f32[2048,2,128]{2,1,0:T(2,128)} %get-tuple-element.269, f32[2048,128]{1,0:T(8,128)S(1)} %bitcast.63, pred[2048,2]{1,0:T(8,128)(4,1)S(1)} %copy-done.2, ...), kind=kLoop, calls=%fused_computation.2.clone.1 | loop fusion | flops 6815744 | bytes 10510337 | tf_op jit(solution)/shard_map/while/body/eval_jaxpr/add | solution.py:57
  211.1 3.9 fusion.26
  215.1 17.5 %fusion.27 = (f32[2048,2,128]{2,1,0:T(2,128)}, f32[2048,2,128]{2,1,0:T(2,128)}) fusion(f32[2048,2,128]{2,1,0:T(2,128)} %get-tuple-element.270, pred[]{:T(512)S(6)} %compare.3, f32[2048,2,128]{2,1,0:T(2,128)} %get-tuple-element.269, f32[2048,128]{1,0:T(8,128)S(1)} %bitcast.63, pred[2048,2]{1,0:T(8,128)(4,1)S(1)} %copy-done.2, ...), kind=kLoop, calls=%fused_computation.2.clone.1 | loop fusion | flops 6815744 | bytes 10510337 | tf_op jit(solution)/shard_map/while/body/eval_jaxpr/add | solution.py:57
  236.1 3.8 convolution_bitcast_fusion.2
  241.7 3.9 fusion.26
  245.6 17.5 %fusion.27 = (f32[2048,2,128]{2,1,0:T(2,128)}, f32[2048,2,128]{2,1,0:T(2,128)}) fusion(f32[2048,2,128]{2,1,0:T(2,128)} %get-tuple-element.270, pred[]{:T(512)S(6)} %compare.3, f32[2048,2,128]{2,1,0:T(2,128)} %get-tuple-element.269, f32[2048,128]{1,0:T(8,128)S(1)} %bitcast.63, pred[2048,2]{1,0:T(8,128)(4,1)S(1)} %copy-done.2, ...), kind=kLoop, calls=%fused_computation.2.clone.1 | loop fusion | flops 6815744 | bytes 10510337 | tf_op jit(solution)/shard_map/while/body/eval_jaxpr/add | solution.py:57
  266.6 3.8 convolution_bitcast_fusion.2
  272.2 3.9 fusion.26
  276.1 17.5 %fusion.27 = (f32[2048,2,128]{2,1,0:T(2,128)}, f32[2048,2,128]{2,1,0:T(2,128)}) fusion(f32[2048,2,128]{2,1,0:T(2,128)} %get-tuple-element.270, pred[]{:T(512)S(6)} %compare.3, f32[2048,2,128]{2,1,0:T(2,128)} %get-tuple-element.269, f32[2048,128]{1,0:T(8,128)S(1)} %bitcast.63, pred[2048,2]{1,0:T(8,128)(4,1)S(1)} %copy-done.2, ...), kind=kLoop, calls=%fused_computation.2.clone.1 | loop fusion | flops 6815744 | bytes 10510337 | tf_op jit(solution)/shard_map/while/body/eval_jaxpr/add | solution.py:57
  297.1 3.8 convolution_bitcast_fusion.2
  302.7 3.9 fusion.26
  306.7 17.5 %fusion.27 = (f32[2048,2,128]{2,1,0:T(2,128)}, f32[2048,2,128]{2,1,0:T(2,128)}) fusion(f32[2048,2,128]{2,1,0:T(2,128)} %get-tuple-element.270, pred[]{:T(512)S(6)} %compare.3, f32[2048,2,128]{2,1,0:T(2,128)} %get-tuple-element.269, f32[2048,128]{1,0:T(8,128)S(1)} %bitcast.63, pred[2048,2]{1,0:T(8,128)(4,1)S(1)} %copy-done.2, ...), kind=kLoop, calls=%fused_computation.2.clone.1 | loop fusion | flops 6815744 | bytes 10510337 | tf_op jit(solution)/shard_map/while/body/eval_jaxpr/add | solution.py:57
  333.3 3.9 fusion.26
  337.2 17.5 %fusion.27 = (f32[2048,2,128]{2,1,0:T(2,128)}, f32[2048,2,128]{2,1,0:T(2,128)}) fusion(f32[2048,2,128]{2,1,0:T(2,128)} %get-tuple-element.270, pred[]{:T(512)S(6)} %compare.3, f32[2048,2,128]{2,1,0:T(2,128)} %get-tuple-element.269, f32[2048,128]{1,0:T(8,128)S(1)} %bitcast.63, pred[2048,2]{1,0:T(8,128)(4,1)S(1)} %copy-done.2, ...), kind=kLoop, calls=%fused_computation.2.clone.1 | loop fusion | flops 6815744 | bytes 10510337 | tf_op jit(solution)/shard_map/while/body/eval_jaxpr/add | solution.py:57
  363.8 3.9 fusion.26
  367.7 17.5 %fusion.27 = (f32[2048,2,128]{2,1,0:T(2,128)}, f32[2048,2,128]{2,1,0:T(2,128)}) fusion(f32[2048,2,128]{2,1,0:T(2,128)} %get-tuple-element.270, pred[]{:T(512)S(6)} %compare.3, f32[2048,2,128]{2,1,0:T(2,128)} %get-tuple-element.269, f32[2048,128]{1,0:T(8,128)S(1)} %bitcast.63, pred[2048,2]{1,0:T(8,128)(4,1)S(1)} %copy-done.2, ...), kind=kLoop, calls=%fused_computation.2.clone.1 | loop fusion | flops 6815744 | bytes 10510337 | tf_op jit(solution)/shard_map/while/body/eval_jaxpr/add | solution.py:57
  394.3 3.9 fusion.26
  398.3 17.5 %fusion.27 = (f32[2048,2,128]{2,1,0:T(2,128)}, f32[2048,2,128]{2,1,0:T(2,128)}) fusion(f32[2048,2,128]{2,1,0:T(2,128)} %get-tuple-element.270, pred[]{:T(512)S(6)} %compare.3, f32[2048,2,128]{2,1,0:T(2,128)} %get-tuple-element.269, f32[2048,128]{1,0:T(8,128)S(1)} %bitcast.63, pred[2048,2]{1,0:T(8,128)(4,1)S(1)} %copy-done.2, ...), kind=kLoop, calls=%fused_computation.2.clone.1 | loop fusion | flops 6815744 | bytes 10510337 | tf_op jit(solution)/shard_map/while/body/eval_jaxpr/add | solution.py:57
  419.3 3.8 convolution_bitcast_fusion.2
  424.9 3.9 fusion.26
  428.8 17.5 %fusion.27 = (f32[2048,2,128]{2,1,0:T(2,128)}, f32[2048,2,128]{2,1,0:T(2,128)}) fusion(f32[2048,2,128]{2,1,0:T(2,128)} %get-tuple-element.270, pred[]{:T(512)S(6)} %compare.3, f32[2048,2,128]{2,1,0:T(2,128)} %get-tuple-element.269, f32[2048,128]{1,0:T(8,128)S(1)} %bitcast.63, pred[2048,2]{1,0:T(8,128)(4,1)S(1)} %copy-done.2, ...), kind=kLoop, calls=%fused_computation.2.clone.1 | loop fusion | flops 6815744 | bytes 10510337 | tf_op jit(solution)/shard_map/while/body/eval_jaxpr/add | solution.py:57
  449.8 3.8 convolution_bitcast_fusion.2
  455.4 3.9 fusion.26
  459.3 17.5 %fusion.27 = (f32[2048,2,128]{2,1,0:T(2,128)}, f32[2048,2,128]{2,1,0:T(2,128)}) fusion(f32[2048,2,128]{2,1,0:T(2,128)} %get-tuple-element.270, pred[]{:T(512)S(6)} %compare.3, f32[2048,2,128]{2,1,0:T(2,128)} %get-tuple-element.269, f32[2048,128]{1,0:T(8,128)S(1)} %bitcast.63, pred[2048,2]{1,0:T(8,128)(4,1)S(1)} %copy-done.2, ...), kind=kLoop, calls=%fused_computation.2.clone.1 | loop fusion | flops 6815744 | bytes 10510337 | tf_op jit(solution)/shard_map/while/body/eval_jaxpr/add | solution.py:57
  485.9 3.9 fusion.26
  489.9 17.5 %fusion.27 = (f32[2048,2,128]{2,1,0:T(2,128)}, f32[2048,2,128]{2,1,0:T(2,128)}) fusion(f32[2048,2,128]{2,1,0:T(2,128)} %get-tuple-element.270, pred[]{:T(512)S(6)} %compare.3, f32[2048,2,128]{2,1,0:T(2,128)} %get-tuple-element.269, f32[2048,128]{1,0:T(8,128)S(1)} %bitcast.63, pred[2048,2]{1,0:T(8,128)(4,1)S(1)} %copy-done.2, ...), kind=kLoop, calls=%fused_computation.2.clone.1 | loop fusion | flops 6815744 | bytes 10510337 | tf_op jit(solution)/shard_map/while/body/eval_jaxpr/add | solution.py:57
  516.5 3.9 fusion.26
  520.4 17.5 %fusion.27 = (f32[2048,2,128]{2,1,0:T(2,128)}, f32[2048,2,128]{2,1,0:T(2,128)}) fusion(f32[2048,2,128]{2,1,0:T(2,128)} %get-tuple-element.270, pred[]{:T(512)S(6)} %compare.3, f32[2048,2,128]{2,1,0:T(2,128)} %get-tuple-element.269, f32[2048,128]{1,0:T(8,128)S(1)} %bitcast.63, pred[2048,2]{1,0:T(8,128)(4,1)S(1)} %copy-done.2, ...), kind=kLoop, calls=%fused_computation.2.clone.1 | loop fusion | flops 6815744 | bytes 10510337 | tf_op jit(solution)/shard_map/while/body/eval_jaxpr/add | solution.py:57
  547.0 3.9 fusion.26
  550.9 17.5 %fusion.27 = (f32[2048,2,128]{2,1,0:T(2,128)}, f32[2048,2,128]{2,1,0:T(2,128)}) fusion(f32[2048,2,128]{2,1,0:T(2,128)} %get-tuple-element.270, pred[]{:T(512)S(6)} %compare.3, f32[2048,2,128]{2,1,0:T(2,128)} %get-tuple-element.269, f32[2048,128]{1,0:T(8,128)S(1)} %bitcast.63, pred[2048,2]{1,0:T(8,128)(4,1)S(1)} %copy-done.2, ...), kind=kLoop, calls=%fused_computation.2.clone.1 | loop fusion | flops 6815744 | bytes 10510337 | tf_op jit(solution)/shard_map/while/body/eval_jaxpr/add | solution.py:57
  577.5 3.9 fusion.26
  581.5 17.5 %fusion.27 = (f32[2048,2,128]{2,1,0:T(2,128)}, f32[2048,2,128]{2,1,0:T(2,128)}) fusion(f32[2048,2,128]{2,1,0:T(2,128)} %get-tuple-element.270, pred[]{:T(512)S(6)} %compare.3, f32[2048,2,128]{2,1,0:T(2,128)} %get-tuple-element.269, f32[2048,128]{1,0:T(8,128)S(1)} %bitcast.63, pred[2048,2]{1,0:T(8,128)(4,1)S(1)} %copy-done.2, ...), kind=kLoop, calls=%fused_computation.2.clone.1 | loop fusion | flops 6815744 | bytes 10510337 | tf_op jit(solution)/shard_map/while/body/eval_jaxpr/add | solution.py:57
  602.4 41.1 %all_to_all.34 = bf16[2048,2,128]{2,1,0:T(2,128)(2,1)S(1)} all-to-all(bf16[2048,2,128]{2,1,0:T(2,128)(2,1)S(1)} %multiply_convert_fusion), channel_id=1, replica_groups=mesh['grp'=2,'skill'=16] {'skill'}, dimensions={0} | all-to-all | bytes 2097152 | tf_op jit(solution)/shard_map/all_to_all | solution.py:64
  (121 shorter events, 146.6 us)
Async XLA Ops:
  0.0 51.0 %copy-start = (bf16[1,16,4,128,128]{4,3,2,1,0:T(8,128)(2,1)S(1)}, bf16[1,16,4,128,128]{4,3,2,1,0:T(8,128)(2,1)}, u32[]{:S(2)}) copy-start(bf16[1,16,4,128,128]{4,3,2,1,0:T(8,128)(2,1)} %param.11) | copy-start | bytes 6291460
  37.5 5.5 copy-start.5
  43.0 7.9 %copy-start.6 = (s32[1,16,4]{1,2,0:T(4,128)S(1)}, s32[1,16,4]{1,2,0:T(4,128)}, u32[]{:S(2)}) copy-start(s32[1,16,4]{1,2,0:T(4,128)} %param.12) | copy-start | bytes 772
  43.0 7.9 %copy-start.7 = (s32[1,16]{1,0:T(1,128)S(1)}, s32[1,16]{1,0:T(1,128)}, u32[]{:S(2)}) copy-start(s32[1,16]{1,0:T(1,128)} %param.13) | copy-start | bytes 196
  46.3 29.2 %collective-permute-start.2 = (bf16[2048,2,128]{2,1,0:T(2,128)(2,1)S(1)}, bf16[2048,2,128]{2,1,0:T(2,128)(2,1)}, u32[]{:S(2)}, u32[]{:S(2)}) collective-permute-start(bf16[2048,2,128]{2,1,0:T(2,128)(2,1)S(1)} %convert_element_type.25), channel_id=1, source_target_pairs={{3,0},{4,1},{5,2},{6,3},{7,4},{8,5},{9,6},{10,7},{11,8},{12,9},{13... | collective-permute-start | bytes 3145736 | tf_op jit(solution)/shard_map/ppermute | solution.py:10
  47.6 45.8 %collective-permute-start.1 = (bf16[2048,2,128]{2,1,0:T(2,128)(2,1)S(1)}, bf16[2048,2,128]{2,1,0:T(2,128)(2,1)}, u32[]{:S(2)}, u32[]{:S(2)}) collective-permute-start(bf16[2048,2,128]{2,1,0:T(2,128)(2,1)S(1)} %convert_element_type.25), channel_id=1, source_target_pairs={{2,0},{3,1},{4,2},{5,3},{6,4},{7,5},{8,6},{9,7},{10,8},{11,9},{12,... | collective-permute-start | bytes 3145736 | tf_op jit(solution)/shard_map/ppermute | solution.py:10
  48.9 46.3 %collective-permute-start = (bf16[2048,2,128]{2,1,0:T(2,128)(2,1)S(1)}, bf16[2048,2,128]{2,1,0:T(2,128)(2,1)}, u32[]{:S(2)}, u32[]{:S(2)}) collective-permute-start(bf16[2048,2,128]{2,1,0:T(2,128)(2,1)S(1)} %convert_element_type.25), channel_id=1, source_target_pairs={{1,0},{2,1},{3,2},{4,3},{5,4},{6,5},{7,6},{8,7},{9,8},{10,9},{11,1... | collective-permute-start | bytes 3145736 | tf_op jit(solution)/shard_map/ppermute | solution.py:10
  54.1 4.2 copy-start.3
  58.3 8.6 %copy-start.4 = (f32[16,2,2048]{2,1,0:T(2,128)S(1)}, f32[16,2,2048]{2,1,0:T(2,128)}, u32[]{:S(2)}) copy-start(f32[16,2,2048]{2,1,0:T(2,128)} %param.15) | copy-start | bytes 786436
  120.2 3.9 copy-start.2
  150.0 3.9 copy-start.2
  180.6 3.9 copy-start.2
  211.1 3.9 copy-start.2
  241.7 3.9 copy-start.2
  272.2 3.9 copy-start.2
  302.7 3.9 copy-start.2
  333.3 3.9 copy-start.2
  363.8 3.9 copy-start.2
  394.3 3.9 copy-start.2
  424.9 3.9 copy-start.2
  455.4 3.9 copy-start.2
  485.9 3.9 copy-start.2
  516.5 3.9 copy-start.2
  547.0 3.9 copy-start.2
  577.5 3.9 copy-start.2
  643.5 2.3 copy-start.1
where the time goes:
time: 649 us; the launch traced here: 646 us
  other arithmetic  327 us (50%)
  local copies, waits for them, and re-layouts  155 us (24%)
  blocking collectives  73.7 us (11%)
  matrix products  65.2 us (10%)
  waiting for transfers between devices  19.7 us (3%)
    add x16, other arithmetic, level_step(): running_total * jnp.exp(running_max - new_max) + jnp.exp(score - new_max)  279 us
    slice x16, local copies, waits for them, and re-layouts, level_step(): cont[:, option:option + 1, :]  62.9 us
    dot_general x16, matrix products, level_step(): jnp.dot(matrix, transit[index], preferred_element_type=jnp.float32)  60.2 us
    all_to_all x1, blocking collectives, on_device(): lax.all_to_all(value_tile, 'skill', split_axis=0, concat_axis=2, tiled=True)  41.1 us
    eq x16, other arithmetic, level_step(): chosen == option  35.3 us
    all_to_all x1, blocking collectives, on_device(): lax.all_to_all(value_next, 'skill', split_axis=2, concat_axis=0, tiled=True)  32.5 us
    dot_general x16, local copies, waits for them, and re-layouts, level_step(): jnp.dot(matrix, transit[index], preferred_element_type=jnp.float32)  28.9 us
    unnamed x18, local copies, waits for them, and re-layouts  26.4 us
  transfers between devices with their start and end apart: 3, of which 2 were waited for; matrix products, arithmetic and copies ran while one was open for 4% of the time, Pallas kernels for 0%

commit v1 on v0

--- a/solution.py
+++ b/solution.py
@@ -21,7 +21,12 @@
     parents = rows // shocks
     blocks = block_offset.shape[-1]
     levels = block_offset.shape[1]
-    arrived = lax.all_to_all(value_next, "skill", split_axis=2, concat_axis=0, tiled=True)
+    arrived = jnp.concatenate(
+        lax.all_to_all(
+            jnp.stack(jnp.split(value_next, lax.axis_size("skill"), axis=2)), "skill", 0, 0
+        ),
+        axis=0,
+    )
     width = arrived.shape[2]
     grid = arrived.astype(jnp.float32).reshape(parents, shocks, assets * width)
     mixed = jnp.einsum("fe,hex->hfx", income_matrix, grid, precision=lax.Precision.HIGHEST)

time: 649 us -> 654 us (level)
    unnamed x18 -> x34, local copies, waits for them, and re-layouts: 26.4 us -> 35.1 us
where the time goes in v1:
time: 654 us; the launch traced here: 651 us
  other arithmetic  326 us (50%)
  local copies, waits for them, and re-layouts  160 us (24%)
  blocking collectives  73.5 us (11%)
  matrix products  65.5 us (10%)
  waiting for transfers between devices  19.9 us (3%)
    add x16, other arithmetic, level_step(): running_total * jnp.exp(running_max - new_max) + jnp.exp(score - new_max)  279 us
    slice x16, local copies, waits for them, and re-layouts, level_step(): cont[:, option:option + 1, :]  62.2 us
    dot_general x16, matrix products, level_step(): jnp.dot(matrix, transit[index], preferred_element_type=jnp.float32)  60.3 us
    all_to_all x1, blocking collectives, on_device(): lax.all_to_all(value_tile, 'skill', split_axis=0, concat_axis=2, tiled=True)  41.1 us
    eq x16, other arithmetic, level_step(): chosen == option  35.3 us
    unnamed x34, local copies, waits for them, and re-layouts  35.1 us
    all_to_all x1, blocking collectives, on_device(): lax.all_to_all(jnp.stack(jnp.split(value_next, lax.axis_size('skill'), ax...  32.3 us
    dot_general x16, local copies, waits for them, and re-layouts, level_step(): jnp.dot(matrix, transit[index], preferred_element_type=jnp.float32)  29.1 us
  transfers between devices with their start and end apart: 3, of which 2 were waited for; matrix products, arithmetic and copies ran while one was open for 4% of the time, Pallas kernels for 0%

profile of v1, /device:TPU:1, one launch (start us, length us, event | category | flops | bytes accessed | tf_op | source)
XLA Modules:
  0.0 650.9 jit_solution(2229547621466272355)
XLA Ops:
  14.6 32.3 %all_to_all.23 = bf16[16,128,2,128]{3,2,1,0:T(2,128)(2,1)S(1)} all-to-all(bf16[16,128,2,128]{3,2,1,0:T(2,128)(2,1)S(1)} %bitcast_dynamic-update-slice_fusion), channel_id=1, replica_groups=mesh['grp'=2,'skill'=16] {'skill'}, dimensions={0} | all-to-all | bytes 2097152 | tf_op jit(solution)/shard_map/all_to_all | solution.py:25
  59.5 4.2 copy.24
  63.7 8.6 %copy.18 = s32[16,2,2048]{1,2,0:T(8,128)} copy(s32[16,2,2048]{2,1,0:T(2,128)S(1)} %copy-done.4) | data formatting | bytes 524288 | tf_op args[5]
  72.3 8.6 %copy.17 = f32[16,2,2048]{1,2,0:T(8,128)} copy(f32[16,2,2048]{2,1,0:T(2,128)S(1)} %copy-done.5) | data formatting | bytes 524288 | tf_op args[6]
  80.9 18.1 %collective-permute-done.1 = bf16[2048,2,128]{2,1,0:T(2,128)(2,1)} collective-permute-done((bf16[2048,2,128]{2,1,0:T(2,128)(2,1)}, bf16[2048,2,128]{2,1,0:T(2,128)(2,1)}, u32[]{:S(2)}, u32[]{:S(2)}) %collective-permute-start.1) | collective-permute-done | bytes 1048608 | tf_op jit(solution)/shard_map/ppermute | solution.py:10
  100.8 8.5 %pad_maximum_fusion = bf16[2048,2,512]{2,1,0:T(2,128)(2,1)} fusion(bf16[2048,2,128]{2,1,0:T(2,128)(2,1)S(1)} %collective-permute-done.2, bf16[2048,2,128]{2,1,0:T(2,128)(2,1)} %collective-permute-done.1, bf16[2048,2,128]{2,1,0:T(2,128)(2,1)} %collective-permute-done, bf16[2048,2,128]{2,1,0:T(2,128)(2,1)S(1)} %copy-done.3), kind=kLoop, calls=%fused_computation.12 | loop fusion | flops 16777216 | bytes 8388608 | tf_op jit(solution)/shard_map/concatenate | solution.py:37
  109.4 7.2 %reshape.74 = bf16[4096,512]{1,0:T(8,128)(2,1)} reshape(bf16[2048,2,512]{2,1,0:T(2,128)(2,1)} %pad_maximum_fusion) | data formatting | bytes 8388608 | tf_op jit(solution)/shard_map/reshape | solution.py:38
  116.6 487.4 %while.16 = (s32[]{:T(128)}, f32[2048,2,128]{2,1,0:T(2,128)}, f32[2048,2,128]{2,1,0:T(2,128)}, f32[16,2048,2,1]{2,1,3,0:T(8,128)}, s32[16,2048,2]{2,1,0:T(8,128)...) while((s32[]{:T(128)}, f32[2048,2,128]{2,1,0:T(2,128)}, ...), condition=%wide.region_1.2_spmd.clone, body=%wide.region_0.1_spmd.clone.sunk | while | flops 543694848 | bytes 25395352 | solution.py:67
  120.0 3.8 convolution_bitcast_fusion.2
  125.6 3.9 fusion.26
  129.5 16.8 %fusion.27 = (f32[2048,2,128]{2,1,0:T(2,128)}, f32[2048,2,128]{2,1,0:T(2,128)}) fusion(f32[2048,2,128]{2,1,0:T(2,128)} %get-tuple-element.256, pred[]{:T(512)S(6)} %compare.3, f32[2048,2,128]{2,1,0:T(2,128)} %get-tuple-element.255, f32[2048,128]{1,0:T(8,128)S(1)} %bitcast.93, pred[2048,2]{1,0:T(8,128)(4,1)S(1)} %copy-done.2, ...), kind=kLoop, calls=%fused_computation.2.clone.1 | loop fusion | flops 6815744 | bytes 10510337 | tf_op jit(solution)/shard_map/while/body/eval_jaxpr/add | solution.py:62
  155.5 3.9 fusion.26
  159.4 17.5 %fusion.27 = (f32[2048,2,128]{2,1,0:T(2,128)}, f32[2048,2,128]{2,1,0:T(2,128)}) fusion(f32[2048,2,128]{2,1,0:T(2,128)} %get-tuple-element.256, pred[]{:T(512)S(6)} %compare.3, f32[2048,2,128]{2,1,0:T(2,128)} %get-tuple-element.255, f32[2048,128]{1,0:T(8,128)S(1)} %bitcast.93, pred[2048,2]{1,0:T(8,128)(4,1)S(1)} %copy-done.2, ...), kind=kLoop, calls=%fused_computation.2.clone.1 | loop fusion | flops 6815744 | bytes 10510337 | tf_op jit(solution)/shard_map/while/body/eval_jaxpr/add | solution.py:62
  180.4 3.8 convolution_bitcast_fusion.2
  186.0 3.9 fusion.26
  189.9 17.5 %fusion.27 = (f32[2048,2,128]{2,1,0:T(2,128)}, f32[2048,2,128]{2,1,0:T(2,128)}) fusion(f32[2048,2,128]{2,1,0:T(2,128)} %get-tuple-element.256, pred[]{:T(512)S(6)} %compare.3, f32[2048,2,128]{2,1,0:T(2,128)} %get-tuple-element.255, f32[2048,128]{1,0:T(8,128)S(1)} %bitcast.93, pred[2048,2]{1,0:T(8,128)(4,1)S(1)} %copy-done.2, ...), kind=kLoop, calls=%fused_computation.2.clone.1 | loop fusion | flops 6815744 | bytes 10510337 | tf_op jit(solution)/shard_map/while/body/eval_jaxpr/add | solution.py:62
  210.9 3.8 convolution_bitcast_fusion.2
  216.5 3.9 fusion.26
  220.4 17.5 %fusion.27 = (f32[2048,2,128]{2,1,0:T(2,128)}, f32[2048,2,128]{2,1,0:T(2,128)}) fusion(f32[2048,2,128]{2,1,0:T(2,128)} %get-tuple-element.256, pred[]{:T(512)S(6)} %compare.3, f32[2048,2,128]{2,1,0:T(2,128)} %get-tuple-element.255, f32[2048,128]{1,0:T(8,128)S(1)} %bitcast.93, pred[2048,2]{1,0:T(8,128)(4,1)S(1)} %copy-done.2, ...), kind=kLoop, calls=%fused_computation.2.clone.1 | loop fusion | flops 6815744 | bytes 10510337 | tf_op jit(solution)/shard_map/while/body/eval_jaxpr/add | solution.py:62
  241.4 3.8 convolution_bitcast_fusion.2
  247.0 3.9 fusion.26
  250.9 17.5 %fusion.27 = (f32[2048,2,128]{2,1,0:T(2,128)}, f32[2048,2,128]{2,1,0:T(2,128)}) fusion(f32[2048,2,128]{2,1,0:T(2,128)} %get-tuple-element.256, pred[]{:T(512)S(6)} %compare.3, f32[2048,2,128]{2,1,0:T(2,128)} %get-tuple-element.255, f32[2048,128]{1,0:T(8,128)S(1)} %bitcast.93, pred[2048,2]{1,0:T(8,128)(4,1)S(1)} %copy-done.2, ...), kind=kLoop, calls=%fused_computation.2.clone.1 | loop fusion | flops 6815744 | bytes 10510337 | tf_op jit(solution)/shard_map/while/body/eval_jaxpr/add | solution.py:62
  271.9 3.8 convolution_bitcast_fusion.2
  277.5 3.9 fusion.26
  281.4 17.5 %fusion.27 = (f32[2048,2,128]{2,1,0:T(2,128)}, f32[2048,2,128]{2,1,0:T(2,128)}) fusion(f32[2048,2,128]{2,1,0:T(2,128)} %get-tuple-element.256, pred[]{:T(512)S(6)} %compare.3, f32[2048,2,128]{2,1,0:T(2,128)} %get-tuple-element.255, f32[2048,128]{1,0:T(8,128)S(1)} %bitcast.93, pred[2048,2]{1,0:T(8,128)(4,1)S(1)} %copy-done.2, ...), kind=kLoop, calls=%fused_computation.2.clone.1 | loop fusion | flops 6815744 | bytes 10510337 | tf_op jit(solution)/shard_map/while/body/eval_jaxpr/add | solution.py:62
  302.4 3.8 convolution_bitcast_fusion.2
  308.0 3.9 fusion.26
  311.9 17.5 %fusion.27 = (f32[2048,2,128]{2,1,0:T(2,128)}, f32[2048,2,128]{2,1,0:T(2,128)}) fusion(f32[2048,2,128]{2,1,0:T(2,128)} %get-tuple-element.256, pred[]{:T(512)S(6)} %compare.3, f32[2048,2,128]{2,1,0:T(2,128)} %get-tuple-element.255, f32[2048,128]{1,0:T(8,128)S(1)} %bitcast.93, pred[2048,2]{1,0:T(8,128)(4,1)S(1)} %copy-done.2, ...), kind=kLoop, calls=%fused_computation.2.clone.1 | loop fusion | flops 6815744 | bytes 10510337 | tf_op jit(solution)/shard_map/while/body/eval_jaxpr/add | solution.py:62
  332.9 3.8 convolution_bitcast_fusion.2
  338.5 3.9 fusion.26
  342.4 17.5 %fusion.27 = (f32[2048,2,128]{2,1,0:T(2,128)}, f32[2048,2,128]{2,1,0:T(2,128)}) fusion(f32[2048,2,128]{2,1,0:T(2,128)} %get-tuple-element.256, pred[]{:T(512)S(6)} %compare.3, f32[2048,2,128]{2,1,0:T(2,128)} %get-tuple-element.255, f32[2048,128]{1,0:T(8,128)S(1)} %bitcast.93, pred[2048,2]{1,0:T(8,128)(4,1)S(1)} %copy-done.2, ...), kind=kLoop, calls=%fused_computation.2.clone.1 | loop fusion | flops 6815744 | bytes 10510337 | tf_op jit(solution)/shard_map/while/body/eval_jaxpr/add | solution.py:62
  369.0 3.9 fusion.26
  372.9 17.5 %fusion.27 = (f32[2048,2,128]{2,1,0:T(2,128)}, f32[2048,2,128]{2,1,0:T(2,128)}) fusion(f32[2048,2,128]{2,1,0:T(2,128)} %get-tuple-element.256, pred[]{:T(512)S(6)} %compare.3, f32[2048,2,128]{2,1,0:T(2,128)} %get-tuple-element.255, f32[2048,128]{1,0:T(8,128)S(1)} %bitcast.93, pred[2048,2]{1,0:T(8,128)(4,1)S(1)} %copy-done.2, ...), kind=kLoop, calls=%fused_computation.2.clone.1 | loop fusion | flops 6815744 | bytes 10510337 | tf_op jit(solution)/shard_map/while/body/eval_jaxpr/add | solution.py:62
  399.5 3.9 fusion.26
  403.4 17.5 %fusion.27 = (f32[2048,2,128]{2,1,0:T(2,128)}, f32[2048,2,128]{2,1,0:T(2,128)}) fusion(f32[2048,2,128]{2,1,0:T(2,128)} %get-tuple-element.256, pred[]{:T(512)S(6)} %compare.3, f32[2048,2,128]{2,1,0:T(2,128)} %get-tuple-element.255, f32[2048,128]{1,0:T(8,128)S(1)} %bitcast.93, pred[2048,2]{1,0:T(8,128)(4,1)S(1)} %copy-done.2, ...), kind=kLoop, calls=%fused_computation.2.clone.1 | loop fusion | flops 6815744 | bytes 10510337 | tf_op jit(solution)/shard_map/while/body/eval_jaxpr/add | solution.py:62
  430.0 3.9 fusion.26
  434.0 17.5 %fusion.27 = (f32[2048,2,128]{2,1,0:T(2,128)}, f32[2048,2,128]{2,1,0:T(2,128)}) fusion(f32[2048,2,128]{2,1,0:T(2,128)} %get-tuple-element.256, pred[]{:T(512)S(6)} %compare.3, f32[2048,2,128]{2,1,0:T(2,128)} %get-tuple-element.255, f32[2048,128]{1,0:T(8,128)S(1)} %bitcast.93, pred[2048,2]{1,0:T(8,128)(4,1)S(1)} %copy-done.2, ...), kind=kLoop, calls=%fused_computation.2.clone.1 | loop fusion | flops 6815744 | bytes 10510337 | tf_op jit(solution)/shard_map/while/body/eval_jaxpr/add | solution.py:62
  460.6 3.9 fusion.26
  464.5 17.5 %fusion.27 = (f32[2048,2,128]{2,1,0:T(2,128)}, f32[2048,2,128]{2,1,0:T(2,128)}) fusion(f32[2048,2,128]{2,1,0:T(2,128)} %get-tuple-element.256, pred[]{:T(512)S(6)} %compare.3, f32[2048,2,128]{2,1,0:T(2,128)} %get-tuple-element.255, f32[2048,128]{1,0:T(8,128)S(1)} %bitcast.93, pred[2048,2]{1,0:T(8,128)(4,1)S(1)} %copy-done.2, ...), kind=kLoop, calls=%fused_computation.2.clone.1 | loop fusion | flops 6815744 | bytes 10510337 | tf_op jit(solution)/shard_map/while/body/eval_jaxpr/add | solution.py:62
  491.1 3.9 fusion.26
  495.0 17.5 %fusion.27 = (f32[2048,2,128]{2,1,0:T(2,128)}, f32[2048,2,128]{2,1,0:T(2,128)}) fusion(f32[2048,2,128]{2,1,0:T(2,128)} %get-tuple-element.256, pred[]{:T(512)S(6)} %compare.3, f32[2048,2,128]{2,1,0:T(2,128)} %get-tuple-element.255, f32[2048,128]{1,0:T(8,128)S(1)} %bitcast.93, pred[2048,2]{1,0:T(8,128)(4,1)S(1)} %copy-done.2, ...), kind=kLoop, calls=%fused_computation.2.clone.1 | loop fusion | flops 6815744 | bytes 10510337 | tf_op jit(solution)/shard_map/while/body/eval_jaxpr/add | solution.py:62
  521.6 3.9 fusion.26
  525.5 17.5 %fusion.27 = (f32[2048,2,128]{2,1,0:T(2,128)}, f32[2048,2,128]{2,1,0:T(2,128)}) fusion(f32[2048,2,128]{2,1,0:T(2,128)} %get-tuple-element.256, pred[]{:T(512)S(6)} %compare.3, f32[2048,2,128]{2,1,0:T(2,128)} %get-tuple-element.255, f32[2048,128]{1,0:T(8,128)S(1)} %bitcast.93, pred[2048,2]{1,0:T(8,128)(4,1)S(1)} %copy-done.2, ...), kind=kLoop, calls=%fused_computation.2.clone.1 | loop fusion | flops 6815744 | bytes 10510337 | tf_op jit(solution)/shard_map/while/body/eval_jaxpr/add | solution.py:62
  552.1 3.9 fusion.26
  556.0 17.5 %fusion.27 = (f32[2048,2,128]{2,1,0:T(2,128)}, f32[2048,2,128]{2,1,0:T(2,128)}) fusion(f32[2048,2,128]{2,1,0:T(2,128)} %get-tuple-element.256, pred[]{:T(512)S(6)} %compare.3, f32[2048,2,128]{2,1,0:T(2,128)} %get-tuple-element.255, f32[2048,128]{1,0:T(8,128)S(1)} %bitcast.93, pred[2048,2]{1,0:T(8,128)(4,1)S(1)} %copy-done.2, ...), kind=kLoop, calls=%fused_computation.2.clone.1 | loop fusion | flops 6815744 | bytes 10510337 | tf_op jit(solution)/shard_map/while/body/eval_jaxpr/add | solution.py:62
  582.6 3.9 fusion.26
  586.5 17.5 %fusion.27 = (f32[2048,2,128]{2,1,0:T(2,128)}, f32[2048,2,128]{2,1,0:T(2,128)}) fusion(f32[2048,2,128]{2,1,0:T(2,128)} %get-tuple-element.256, pred[]{:T(512)S(6)} %compare.3, f32[2048,2,128]{2,1,0:T(2,128)} %get-tuple-element.255, f32[2048,128]{1,0:T(8,128)S(1)} %bitcast.93, pred[2048,2]{1,0:T(8,128)(4,1)S(1)} %copy-done.2, ...), kind=kLoop, calls=%fused_computation.2.clone.1 | loop fusion | flops 6815744 | bytes 10510337 | tf_op jit(solution)/shard_map/while/body/eval_jaxpr/add | solution.py:62
  607.4 41.1 %all_to_all.24 = bf16[2048,2,128]{2,1,0:T(2,128)(2,1)S(1)} all-to-all(bf16[2048,2,128]{2,1,0:T(2,128)(2,1)S(1)} %multiply_convert_fusion), channel_id=1, replica_groups=mesh['grp'=2,'skill'=16] {'skill'}, dimensions={0} | all-to-all | bytes 2097152 | tf_op jit(solution)/shard_map/all_to_all | solution.py:69
  (137 shorter events, 153.6 us)
Async XLA Ops:
  0.0 56.4 %copy-start = (bf16[1,16,4,128,128]{4,3,2,1,0:T(8,128)(2,1)S(1)}, bf16[1,16,4,128,128]{4,3,2,1,0:T(8,128)(2,1)}, u32[]{:S(2)}) copy-start(bf16[1,16,4,128,128]{4,3,2,1,0:T(8,128)(2,1)} %param.11) | copy-start | bytes 6291460
  14.6 33.8 %copy-start.6 = (f32[32,32]{1,0:T(8,128)S(1)}, f32[32,32]{1,0:T(8,128)}, u32[]{:S(2)}) copy-start(f32[32,32]{1,0:T(8,128)} %param.10) | copy-start | bytes 12292
  48.4 7.9 %copy-start.7 = (s32[1,16,4]{1,2,0:T(4,128)S(1)}, s32[1,16,4]{1,2,0:T(4,128)}, u32[]{:S(2)}) copy-start(s32[1,16,4]{1,2,0:T(4,128)} %param.12) | copy-start | bytes 772
  48.4 8.0 %copy-start.8 = (s32[1,16]{1,0:T(1,128)S(1)}, s32[1,16]{1,0:T(1,128)}, u32[]{:S(2)}) copy-start(s32[1,16]{1,0:T(1,128)} %param.13) | copy-start | bytes 196
  51.7 29.2 %collective-permute-start.2 = (bf16[2048,2,128]{2,1,0:T(2,128)(2,1)}, bf16[2048,2,128]{2,1,0:T(2,128)(2,1)S(1)}, u32[]{:S(2)}, u32[]{:S(2)}) collective-permute-start(bf16[2048,2,128]{2,1,0:T(2,128)(2,1)} %convert_element_type.25), channel_id=1, source_target_pairs={{3,0},{4,1},{5,2},{6,3},{7,4},{8,5},{9,6},{10,7},{11,8},{12,9},{13... | collective-permute-start | bytes 3145736 | tf_op jit(solution)/shard_map/ppermute | solution.py:10
  53.0 46.0 %collective-permute-start.1 = (bf16[2048,2,128]{2,1,0:T(2,128)(2,1)}, bf16[2048,2,128]{2,1,0:T(2,128)(2,1)}, u32[]{:S(2)}, u32[]{:S(2)}) collective-permute-start(bf16[2048,2,128]{2,1,0:T(2,128)(2,1)} %convert_element_type.25), channel_id=1, source_target_pairs={{2,0},{3,1},{4,2},{5,3},{6,4},{7,5},{8,6},{9,7},{10,8},{11,9},{12,... | collective-permute-start | bytes 3145736 | tf_op jit(solution)/shard_map/ppermute | solution.py:10
  54.3 46.5 %collective-permute-start = (bf16[2048,2,128]{2,1,0:T(2,128)(2,1)}, bf16[2048,2,128]{2,1,0:T(2,128)(2,1)}, u32[]{:S(2)}, u32[]{:S(2)}) collective-permute-start(bf16[2048,2,128]{2,1,0:T(2,128)(2,1)} %convert_element_type.25), channel_id=1, source_target_pairs={{1,0},{2,1},{3,2},{4,3},{5,4},{6,5},{7,6},{8,7},{9,8},{10,9},{11,1... | collective-permute-start | bytes 3145736 | tf_op jit(solution)/shard_map/ppermute | solution.py:10
  59.5 4.2 copy-start.4
  63.7 8.6 %copy-start.5 = (f32[16,2,2048]{2,1,0:T(2,128)S(1)}, f32[16,2,2048]{2,1,0:T(2,128)}, u32[]{:S(2)}) copy-start(f32[16,2,2048]{2,1,0:T(2,128)} %param.15) | copy-start | bytes 786436
  72.3 28.5 %copy-start.3 = (bf16[2048,2,128]{2,1,0:T(2,128)(2,1)S(1)}, bf16[2048,2,128]{2,1,0:T(2,128)(2,1)}, u32[]{:S(2)}) copy-start(bf16[2048,2,128]{2,1,0:T(2,128)(2,1)} %convert_element_type.25) | copy-start | bytes 3145732
  125.6 3.9 copy-start.2
  155.5 3.9 copy-start.2
  186.0 3.9 copy-start.2
  216.5 3.9 copy-start.2
  247.0 3.9 copy-start.2
  277.5 3.9 copy-start.2
  308.0 3.9 copy-start.2
  338.5 3.9 copy-start.2
  369.0 3.9 copy-start.2
  399.5 3.9 copy-start.2
  430.0 3.9 copy-start.2
  460.6 3.9 copy-start.2
  491.1 3.9 copy-start.2
  521.6 3.9 copy-start.2
  552.1 3.9 copy-start.2
  582.6 3.9 copy-start.2
  648.5 2.3 copy-start.1
